TPU v7x, 32 devices: a whole 2x2x4 slice. The times are simulated.
32 devices in a mesh: parts: 2 (over y), row: 4 (over z), col: 4 (over x, core).
Axes of the slice: x: 2, y: 2, z: 4, core: 2. Of those that a mesh axis runs over, the one named last changes fastest.
Arguments:
- sigma_anc: float32 [24576, 12288], P(('parts', 'row'), 'col'), parts along dimension 0
- normal_factor: float32 [4, 12288, 512], P('parts', ('col', 'row')), parts along dimension 0, may hold values from -0.078125 to 0.078125
- jj_inverse: float32 [4, 512, 512], P('parts', None, 'col'), parts along dimension 0, may hold values from -6 to 6
- blocks: int32 [4, 128], P('parts'), parts along dimension 0, may hold values from 0 to 255, as said below
Outputs:
- sigma_rj: float32 [4, 12288, 512], P('parts', 'row', 'col'), parts along dimension 0
- sigma_jj: float32 [4, 512, 512], P('parts', None, 'col'), parts along dimension 0
There are 2 independent parts, one for each index of `parts`. A program takes and returns all parts, laid end to end along the dimension named above; each array names one. Nothing has to cross between parts.
Inputs may be any that keep to these rules, and one draw needn't show every extreme that they name: Each list names 128 different blocks and always holds block 0 and block 255.
All inputs are finite; a program needn't handle non-finite values.
Results may differ from a plain program's by a relative error of at most 0.0001.
Values sent between devices are 32-bit elements; how exact they have to be, the bound alone decides.
A program may use at most 192 MiB of HBM per device.

v0:
```python
import jax
import jax.numpy as jnp
from jax import lax
from jax.sharding import PartitionSpec as P

BLK = 48


def broadcast(value, axis, source):
    kept = jnp.where(lax.axis_index(axis) == source, value, 0).astype(value.dtype)
    return lax.psum(kept, axis)


def listed_mask(blocks, first_block, count, rows):
    block_ids = first_block + jnp.arange(count, dtype=jnp.int32)
    listed = jnp.any(blocks[:, :, None] == block_ids[None, None, :], axis=1).astype(jnp.float32)
    return jnp.repeat(listed, BLK, axis=1, total_repeat_length=rows)[:, :, None]


def shards(sigma_anc, normal_factor, jj_inverse, blocks):
    tile_rows, tile_cols = sigma_anc.shape
    row_count = lax.axis_size("row")
    row_index = lax.axis_index("row")
    col_index = lax.axis_index("col")
    local_rows = normal_factor.shape[1]
    local_blocks = local_rows // BLK
    first_local = (col_index * row_count + row_index) * local_blocks
    masked = normal_factor * listed_mask(blocks, first_local, local_blocks, local_rows)
    row_blocks = tile_rows // BLK
    row_mask = listed_mask(blocks, row_index * row_blocks, row_blocks, tile_rows)
    start_row = row_index * tile_rows
    root_col = start_row // tile_cols
    offset = jnp.clip(start_row - col_index * tile_cols, 0, tile_cols - tile_rows)
    partial_list = []
    slab_list = []
    for supernode in range(2):
        gathered = lax.all_gather(masked[supernode], "row", axis=0, tiled=True)
        partial_list.append(
            jnp.dot(
                sigma_anc,
                gathered,
                precision=lax.Precision.HIGHEST,
                preferred_element_type=jnp.float32,
            )
        )
        slab_list.append(lax.dynamic_slice_in_dim(gathered, offset, tile_rows, 0))
    partials = jnp.stack(partial_list)
    slabs = jnp.stack(slab_list)
    summed = lax.psum(partials, "col")
    full_rj = -(summed * row_mask)
    part_cols = jj_inverse.shape[2]
    sigma_rj = lax.dynamic_slice_in_dim(full_rj, col_index * part_cols, part_cols, 2)
    owner_rows = broadcast(slabs, "col", root_col)
    update = jnp.einsum("srw,srv->swv", owner_rows, sigma_rj, precision=lax.Precision.HIGHEST)
    sigma_jj = jj_inverse - lax.psum(update, "row")
    return (sigma_rj, sigma_jj)


def solution(mesh):
    placed = (
        P(("parts", "row"), "col"),
        P("parts", ("col", "row"), None),
        P("parts", None, "col"),
        P("parts", None),
    )
    return jax.shard_map(
        shards,
        mesh=mesh,
        in_specs=placed,
        out_specs=(P("parts", "row", "col"), P("parts", None, "col")),
        check_vma=False,
    )
```

profile of v0, /device:TPU:0, one launch (start us, length us, event | category | flops | bytes accessed | tf_op | source)
XLA Modules:
  0.0 816.3 jit_solution(12783318977597875389)
XLA Ops:
  7.2 0.0 all-gather.5.cloned.1.call-start
  7.2 0.9 compare_reduce_fusion.1
  8.1 0.1 copy.11
  8.2 0.7 pad_clamp_fusion
  8.9 1.6 gather_fusion
  10.5 0.1 copy.12
  10.6 2.4 copy.13
  13.0 0.2 broadcast_multiply_fusion
  13.2 1.9 fusion.11
  15.1 0.0 all-gather.5.cloned.1.call-update
  15.1 0.0 all-gather.7.cloned.1.call-start
  15.2 0.7 all-gather.7.cloned.1.call-update
  15.9 0.0 all-reduce.6.cloned.1.call-start
  16.0 117.4 %all-gather.5.cloned.1.call-done = f32[1,3072,512]{1,2,0:T(8,128)} async-done(((f32[1,768,512]{1,2,0:T(8,128)}), f32[1,3072,512]{1,2,0:T(8,128)}) %all-gather.5.cloned.1.call-update) | async-done | bytes 6291472 | tf_op jit(solution)/shard_map/all_gather | solution.py:37
  133.3 67.8 %fusion.4 = f32[1,3072,512]{1,2,0:T(8,128)} fusion(f32[3072,3072]{1,0:T(8,128)} %param.8, f32[1,3072,512]{1,2,0:T(8,128)} %all-gather.5.cloned.1.call-done), kind=kOutput, calls=%fused_computation.8 | convolution fusion | flops 57982058496 | bytes 50331648 | tf_op jit(solution)/shard_map/dot_general | solution.py:39
  201.1 47.4 %all-gather.7.cloned.1.call-done = f32[1,3072,512]{1,2,0:T(8,128)} async-done(((f32[1,768,512]{1,2,0:T(8,128)}), f32[1,3072,512]{1,2,0:T(8,128)}) %all-gather.7.cloned.1.call-update) | async-done | bytes 6291472 | tf_op jit(solution)/shard_map/all_gather | solution.py:37
  248.5 68.0 %fusion.7 = f32[1,3072,512]{1,2,0:T(8,128)} fusion(f32[3072,3072]{1,0:T(8,128)} %param.8, f32[1,3072,512]{1,2,0:T(8,128)} %all-gather.7.cloned.1.call-done), kind=kOutput, calls=%fused_computation.9 | convolution fusion | flops 57982058496 | bytes 50331648 | tf_op jit(solution)/shard_map/dot_general | solution.py:39
  316.5 14.6 %pad_maximum_fusion = (f32[2,3072,512]{1,2,0:T(8,128)}, f32[2,3072,512]{1,2,0:T(8,128)}) fusion(f32[1,3072,512]{1,2,0:T(8,128)} %fusion.7, f32[1,3072,512]{1,2,0:T(8,128)} %fusion.4, f32[1,3072,512]{1,2,0:T(8,128)S(1)} %copy-done.1, f32[1,3072,512]{1,2,0:T(8,128)S(1)} %copy-done, pred[]{:T(512)S(6)} %eq.35), kind=kLoop, calls=%fused_computation.2 | loop fusion | flops 9437184 | bytes 50331648 | tf_op jit(solution)/shard_map/stack | solution.py:47
  331.0 0.0 all-reduce.6.cloned.1.call-update
  331.0 0.0 all-reduce.4.cloned.1.call-start
  331.1 0.6 copy-done.3
  331.7 0.2 compare_reduce_fusion
  331.9 0.1 copy.14
  332.0 8.1 gather_fusion.1
  340.1 0.5 copy.15
  340.6 412.4 %all-reduce.6.cloned.1.call-done = (f32[2,3072,512]{1,2,0:T(8,128)}, f32[2,3072,512]{1,2,0:T(8,128)}) async-done(((f32[2,3072,512]{1,2,0:T(8,128)}, f32[2,3072,512]{1,2,0:T(8,128)}), (f32[2,3072,512]{1,2,0:T(8,128)}, f32[2,3072,512]{1,2,0:T(8,128)})) %all-reduce.6.cloned.1.call-update) | async-done | bytes 25165840 | tf_op jit(solution)/shard_map/psum | solution.py:49
  753.0 2.2 fusion.10
  755.2 13.8 %fusion.12 = f32[2,512,128]{2,1,0:T(8,128)} fusion(f32[2,3072,512]{1,2,0:T(8,128)} %get-tuple-element.31, f32[2,3072,128]{1,2,0:T(8,128)S(1)} %fusion.10), kind=kOutput, calls=%fused_computation.20 | convolution fusion | flops 4831838208 | bytes 16252928 | tf_op jit(solution)/shard_map/srw,srv->swv/dot_general | solution.py:54
  769.1 0.0 all-reduce.4.cloned.1.call-update
  769.1 2.4 copy.17
  771.4 36.3 %all-reduce.4.cloned.1.call-done = f32[2,512,128]{2,1,0:T(8,128)} async-done(((f32[2,512,128]{2,1,0:T(8,128)}), f32[2,512,128]{2,1,0:T(8,128)}) %all-reduce.4.cloned.1.call-update) | async-done | bytes 524304 | tf_op jit(solution)/shard_map/psum | solution.py:55
  807.7 2.0 sub.7
  (12 shorter events, 0.0 us)
Async XLA Ops:
  7.2 126.2 %all-gather.5.cloned.1.call-start = ((), (), s32[]{:S(2)}) async-start(), calls=%async_computation.1 | async-start | bytes 7864320 | tf_op jit(solution)/shard_map/all_gather | solution.py:37
  15.1 233.3 %all-gather.7.cloned.1.call-start = ((), (), s32[]{:S(2)}) async-start(), calls=%async_computation.2 | async-start | bytes 7864320 | tf_op jit(solution)/shard_map/all_gather | solution.py:37
  15.9 737.1 %all-reduce.6.cloned.1.call-start = ((), (), s32[]{:S(2)}) async-start(), calls=%async_computation.3 | async-start | bytes 50331648 | tf_op jit(solution)/shard_map/psum | solution.py:49
  248.5 68.0 %copy-start = (f32[1,3072,512]{1,2,0:T(8,128)S(1)}, f32[1,3072,512]{1,2,0:T(8,128)}, u32[]{:S(2)}) copy-start(f32[1,3072,512]{1,2,0:T(8,128)} %all-gather.5.cloned.1.call-done) | copy-start | bytes 18874372
  248.5 68.0 %copy-start.1 = (f32[1,3072,512]{1,2,0:T(8,128)S(1)}, f32[1,3072,512]{1,2,0:T(8,128)}, u32[]{:S(2)}) copy-start(f32[1,3072,512]{1,2,0:T(8,128)} %all-gather.7.cloned.1.call-done) | copy-start | bytes 18874372
  331.0 0.7 copy-start.3
  331.0 1.0 copy-start.2
  331.0 476.7 %all-reduce.4.cloned.1.call-start = ((), (), s32[]{:S(2)}) async-start(), calls=%async_computation | async-start | bytes 1048576 | tf_op jit(solution)/shard_map/psum | solution.py:55
Sparse Core Ops, SparseCore 0:
  15.3 118.0 all-gather.4
  134.9 113.5 all-gather.6
  331.2 421.7 all-reduce.5
  769.2 38.4 all-reduce.3
where the time goes:
time: 817 us; the launch traced here: 816 us
  waiting for transfers between devices  614 us (75%)
  matrix products  150 us (18%)
  other arithmetic  20.8 us (3%)
  local copies, waits for them, and re-layouts  17.7 us (2%)
  between operations  13.9 us (2%)
    psum x1, waiting for transfers between devices, shards(): summed = lax.psum(partials, 'col')  412 us
    all_gather x2, waiting for transfers between devices, shards(): gathered = lax.all_gather(masked[supernode], 'row', axis=0, tiled=True)  165 us
    dot_general x2, matrix products, shards(): jnp.dot(sigma_anc, gathered, precision=lax.Precision.HIGHEST, preferred_e...  136 us
    psum x1, waiting for transfers between devices, shards(): sigma_jj = jj_inverse - lax.psum(update, 'row')  36.3 us
  transfers between devices with their start and end apart: 4, of which 4 were waited for; matrix products, arithmetic and copies ran while one was open for 10% of the time, Pallas kernels for 0%

commit v1 on v0

--- a/solution.py
+++ b/solution.py
@@ -1,9 +1,27 @@
+import functools
 import jax
 import jax.numpy as jnp
 from jax import lax
 from jax.sharding import PartitionSpec as P
+from jax.lax import axis_size, ppermute
 
 BLK = 48
+
+
+def expand_bars_over_axis(obj, named_axis):
+    n = axis_size(named_axis)
+    v_next, big = (obj, 0)
+    while 1 << big < n:
+        series = []
+        for b in tuple(range(n)):
+            series.append((b, b ^ 1 << big))
+        near = ppermute(v_next, axis_name=named_axis, perm=series)
+        v_next = v_next + near
+        big = big + 1
+    return v_next
+
+
+_measure_points = functools.partial(expand_bars_over_axis, named_axis="col")
 
 
 def broadcast(value, axis, source):
@@ -46,7 +64,7 @@
         slab_list.append(lax.dynamic_slice_in_dim(gathered, offset, tile_rows, 0))
     partials = jnp.stack(partial_list)
     slabs = jnp.stack(slab_list)
-    summed = lax.psum(partials, "col")
+    summed = _measure_points(partials)
     full_rj = -(summed * row_mask)
     part_cols = jj_inverse.shape[2]
     sigma_rj = lax.dynamic_slice_in_dim(full_rj, col_index * part_cols, part_cols, 2)

time: 817 us -> 891 us (1.091)
  waiting for transfers between devices: 614 us -> 671 us
  other arithmetic: 20.8 us -> 36.3 us
    ppermute x0 -> x2, waiting for transfers between devices: none -> 472 us  [expand_bars_over_axis(): near = ppermute(v_next, axis_name=named_axis, perm=series)]
    psum x1, waiting for transfers between devices: 412 us -> 0.02 us  [broadcast(): return lax.psum(kept, axis)]
    select_n x0 -> x1, other arithmetic: none -> 11.6 us  [broadcast(): jnp.where(lax.axis_index(axis) == source, value, 0).astype(value.dtype)]
  transfers between devices with their start and end apart: 4 -> 6, of which waited for: 4 -> 5; matrix products, arithmetic and copies ran while one was open for 10% -> 11% of each run, Pallas kernels for 0% -> 0%
where the time goes in v1:
time: 891 us; the launch traced here: 890 us
  waiting for transfers between devices  671 us (75%)
  matrix products  149 us (17%)
  other arithmetic  36.3 us (4%)
  local copies, waits for them, and re-layouts  17.7 us (2%)
  between operations  13.9 us (2%)
    ppermute x2, waiting for transfers between devices, expand_bars_over_axis(): near = ppermute(v_next, axis_name=named_axis, perm=series)  472 us
    all_gather x2, waiting for transfers between devices, shards(): gathered = lax.all_gather(masked[supernode], 'row', axis=0, tiled=True)  165 us
    dot_general x2, matrix products, shards(): jnp.dot(sigma_anc, gathered, precision=lax.Precision.HIGHEST, preferred_e...  136 us
    psum x1, waiting for transfers between devices, shards(): sigma_jj = jj_inverse - lax.psum(update, 'row')  34.3 us
  transfers between devices with their start and end apart: 6, of which 5 were waited for; matrix products, arithmetic and copies ran while one was open for 11% of the time, Pallas kernels for 0%

profile of v1, /device:TPU:0, one launch (start us, length us, event | category | flops | bytes accessed | tf_op | source)
XLA Modules:
  0.0 890.4 jit_solution(11378581451474894549)
XLA Ops:
  7.2 0.9 compare_reduce_fusion.1
  8.1 0.1 copy.11
  8.2 0.7 pad_clamp_fusion
  8.9 1.6 gather_fusion
  10.5 0.1 copy.12
  10.6 2.4 copy.13
  13.0 0.2 broadcast_multiply_fusion
  13.2 1.9 fusion.13
  15.1 0.0 all-gather.7.cloned.1.call-start
  15.2 0.7 all-gather.7.cloned.1.call-update
  15.9 117.4 %all-gather.5.cloned.1.call-done = f32[1,3072,512]{1,2,0:T(8,128)} async-done(((f32[1,768,512]{1,2,0:T(8,128)}), f32[1,3072,512]{1,2,0:T(8,128)}) %all-gather.5.cloned.1.call-update) | async-done | bytes 6291472 | tf_op jit(solution)/shard_map/all_gather | solution.py:55
  133.3 67.8 %fusion.4 = f32[1,3072,512]{1,2,0:T(8,128)} fusion(f32[3072,3072]{1,0:T(8,128)} %param.8, f32[1,3072,512]{1,2,0:T(8,128)} %all-gather.5.cloned.1.call-done), kind=kOutput, calls=%fused_computation.8 | convolution fusion | flops 57982058496 | bytes 50331648 | tf_op jit(solution)/shard_map/dot_general | solution.py:57
  201.1 47.4 %all-gather.7.cloned.1.call-done = f32[1,3072,512]{1,2,0:T(8,128)} async-done(((f32[1,768,512]{1,2,0:T(8,128)}), f32[1,3072,512]{1,2,0:T(8,128)}) %all-gather.7.cloned.1.call-update) | async-done | bytes 6291472 | tf_op jit(solution)/shard_map/all_gather | solution.py:55
  248.5 67.8 %fusion.7 = f32[1,3072,512]{1,2,0:T(8,128)} fusion(f32[3072,3072]{1,0:T(8,128)} %param.8, f32[1,3072,512]{1,2,0:T(8,128)} %all-gather.7.cloned.1.call-done), kind=kOutput, calls=%fused_computation.9 | convolution fusion | flops 57982058496 | bytes 50331648 | tf_op jit(solution)/shard_map/dot_general | solution.py:57
  316.3 8.6 pad_maximum_fusion
  324.9 0.1 collective-permute-start
  324.9 19.3 %collective-permute-done = f32[2,3072,512]{1,2,0:T(8,128)S(1)} collective-permute-done((f32[2,3072,512]{1,2,0:T(8,128)}, f32[2,3072,512]{1,2,0:T(8,128)S(1)}, u32[]{:S(2)}, u32[]{:S(2)}) %collective-permute-start) | collective-permute-done | bytes 12582944 | tf_op jit(solution)/shard_map/ppermute | solution.py:18
  344.2 8.8 fusion.12
  353.0 1.5 collective-permute-start.1
  354.4 11.6 %maximum_select_fusion = f32[2,3072,512]{1,2,0:T(8,128)} fusion(f32[1,3072,512]{1,2,0:T(8,128)} %all-gather.7.cloned.1.call-done, f32[1,3072,512]{1,2,0:T(8,128)} %all-gather.5.cloned.1.call-done, pred[]{:T(512)S(6)} %eq.35), kind=kLoop, calls=%fused_computation.3 | loop fusion | flops 6291456 | bytes 25165824 | tf_op jit(solution)/shard_map/jit(_where)/select_n | solution.py:28
  366.1 0.0 all-reduce.5.cloned.1.call-start
  366.1 0.6 copy-done.2
  366.7 0.2 compare_reduce_fusion
  366.9 0.1 copy.14
  367.0 8.1 gather_fusion.1
  375.2 0.5 copy.15
  375.6 452.3 %collective-permute-done.1 = f32[2,3072,512]{1,2,0:T(8,128)} collective-permute-done((f32[2,3072,512]{1,2,0:T(8,128)}, f32[2,3072,512]{1,2,0:T(8,128)}, u32[]{:S(2)}, u32[]{:S(2)}) %collective-permute-start.1) | collective-permute-done | bytes 12582944 | tf_op jit(solution)/shard_map/ppermute | solution.py:18
  827.9 3.4 fusion.11
  831.4 13.9 %fusion.14 = f32[2,512,128]{2,1,0:T(8,128)} fusion(f32[2,3072,512]{1,2,0:T(8,128)} %all-reduce.3.cloned.1.call-done, f32[2,3072,128]{1,2,0:T(8,128)S(1)} %fusion.11), kind=kOutput, calls=%fused_computation.22 | convolution fusion | flops 4831838208 | bytes 16252928 | tf_op jit(solution)/shard_map/srw,srv->swv/dot_general | solution.py:72
  845.2 2.4 copy.17
  847.6 34.3 %all-reduce.5.cloned.1.call-done = f32[2,512,128]{2,1,0:T(8,128)} async-done(((f32[2,512,128]{2,1,0:T(8,128)}), f32[2,512,128]{2,1,0:T(8,128)}) %all-reduce.5.cloned.1.call-update) | async-done | bytes 524304 | tf_op jit(solution)/shard_map/psum | solution.py:73
  881.9 2.0 sub.7
  (16 shorter events, 0.2 us)
Async XLA Ops:
  7.2 126.1 %all-gather.5.cloned.1.call-start = ((), (), s32[]{:S(2)}) async-start(), calls=%async_computation.2 | async-start | bytes 7864320 | tf_op jit(solution)/shard_map/all_gather | solution.py:55
  15.1 233.3 %all-gather.7.cloned.1.call-start = ((), (), s32[]{:S(2)}) async-start(), calls=%async_computation.3 | async-start | bytes 7864320 | tf_op jit(solution)/shard_map/all_gather | solution.py:55
  15.9 815.5 %all-reduce.3.cloned.1.call-start = ((), (), s32[]{:S(2)}) async-start(), calls=%async_computation | async-start | bytes 25165824 | tf_op jit(solution)/shard_map/psum | solution.py:29
  248.4 67.8 %copy-start = (f32[1,3072,512]{1,2,0:T(8,128)S(1)}, f32[1,3072,512]{1,2,0:T(8,128)}, u32[]{:S(2)}) copy-start(f32[1,3072,512]{1,2,0:T(8,128)} %fusion.4) | copy-start | bytes 18874372
  324.9 19.4 %collective-permute-start = (f32[2,3072,512]{1,2,0:T(8,128)}, f32[2,3072,512]{1,2,0:T(8,128)S(1)}, u32[]{:S(2)}, u32[]{:S(2)}) collective-permute-start(f32[2,3072,512]{1,2,0:T(8,128)} %pad_maximum_fusion), channel_id=1, source_target_pairs={{0,1},{1,0},{2,3},{3,2},{4,5},{5,4},{6,7},{7,6},{8,9},{9,8},{10,11... | collective-permute-start | bytes 37748744 | tf_op jit(solution)/shard_map/ppermute | solution.py:18
  353.0 474.9 %collective-permute-start.1 = (f32[2,3072,512]{1,2,0:T(8,128)}, f32[2,3072,512]{1,2,0:T(8,128)}, u32[]{:S(2)}, u32[]{:S(2)}) collective-permute-start(f32[2,3072,512]{1,2,0:T(8,128)} %fusion.12), channel_id=1, source_target_pairs={{0,2},{1,3},{2,0},{3,1},{4,6},{5,7},{6,4},{7,5},{8,10},{9,11},{10,... | collective-permute-start | bytes 37748744 | tf_op jit(solution)/shard_map/ppermute | solution.py:18
  366.0 0.7 copy-start.2
  366.0 1.0 copy-start.1
  366.1 515.8 %all-reduce.5.cloned.1.call-start = ((), (), s32[]{:S(2)}) async-start(), calls=%async_computation.1 | async-start | bytes 1048576 | tf_op jit(solution)/shard_map/psum | solution.py:73
Sparse Core Ops, SparseCore 0:
  15.2 118.0 all-gather.4
  134.9 113.5 all-gather.6
  366.2 420.4 all-reduce.2
  845.3 36.4 all-reduce.4
